TPU v7x, 32 devices: a whole 2x2x4 slice. The times are simulated.
32 devices in a mesh: seq: 8 (over z, x), tensor: 4 (over y, core).
Axes of the slice: x: 2, y: 2, z: 4, core: 2. Of those that a mesh axis runs over, the one named last changes fastest.
Arguments:
- latents: bfloat16 [1024, 2560], P('seq'), may hold values from -6 to 6
- levels: int32 [8], P('seq'), may hold values from 0 to 999
- head_slot: int32 [1], replicated, may hold values from 0 to 7
- fresh_noise: bfloat16 [128, 2560], P(None, 'tensor'), may hold values from -6 to 6
- ada_weight: bfloat16 [256, 3, 2560], P(None, None, 'tensor'), may hold values from -0.375 to 0.375
- qkv_weight: bfloat16 [2560, 3, 1536], P(None, None, 'tensor'), may hold values from -0.125 to 0.125
- q_gain: float32 [128], replicated, may hold values from 0.5 to 2.5
- k_gain: float32 [128], replicated, may hold values from 0.5 to 2.5
- out_weight: bfloat16 [1536, 2560], P('tensor'), may hold values from -0.15625 to 0.15625
Outputs:
- window: bfloat16 [1024, 2560], P('seq', 'tensor')
- clean: bfloat16 [128, 2560], P('seq', 'tensor')
All inputs are finite; a program needn't handle non-finite values.
Results may differ from a plain program's by a relative error of at most 0.0053.
Values may be sent and summed in bfloat16 or wider, within the bound.
A program may use at most 64 MiB of HBM per device.

v0:
```python
import math

import jax
import jax.numpy as jnp
from jax import lax
from jax.sharding import PartitionSpec as P


def spread(shard, axis, root):
    mine = lax.axis_index(axis) == root
    return lax.psum(jnp.where(mine, shard, jnp.zeros_like(shard)), axis)


def modulation_part(levels, ada_weight):
    embed_width = ada_weight.shape[0]
    half_width = embed_width // 2
    frequency = jnp.exp(-math.log(10000.0) * jnp.arange(half_width, dtype=jnp.float32) / half_width)
    angles = levels.astype(jnp.float32)[:, None] * frequency[None, :]
    embedding = jax.nn.silu(jnp.concatenate([jnp.cos(angles), jnp.sin(angles)], axis=1)).astype(
        jnp.bfloat16
    )
    flat = jnp.dot(
        embedding, ada_weight.reshape(embed_width, -1), preferred_element_type=jnp.float32
    )
    return flat.reshape(3, -1)


def modulate(states, offset_terms, scale_terms):
    average = jnp.mean(states, axis=-1, keepdims=True)
    centered = states - average
    variance = jnp.mean(centered * centered, axis=-1, keepdims=True)
    normed = centered * lax.rsqrt(variance + 1e-06)
    return (normed * (1.0 + scale_terms) + offset_terms).astype(jnp.bfloat16)


def rms_scaled(matrix, gain_vector, factor):
    power = jnp.mean(matrix * matrix, axis=-1, keepdims=True)
    return (matrix * lax.rsqrt(power + 1e-06) * gain_vector * factor).astype(jnp.bfloat16)


def project(hidden, qkv_weight, q_gain, k_gain):
    head_size = q_gain.shape[0]
    projected_all = jnp.dot(
        hidden, qkv_weight.reshape(qkv_weight.shape[0], -1), preferred_element_type=jnp.float32
    )
    projected_all = projected_all.reshape(hidden.shape[0], 3, -1, head_size)
    queries = rms_scaled(projected_all[:, 0], q_gain, 1.0 / math.sqrt(head_size))
    keys = rms_scaled(projected_all[:, 1], k_gain, 1.0)
    values = projected_all[:, 2].astype(jnp.bfloat16)
    return (queries, keys, values)


def attend(queries, query_rank, keys, values, oldest, block_rows, block_count):
    row_count = queries.shape[0]
    head_count = queries.shape[1]
    head_size = queries.shape[2]
    initial = (
        jnp.zeros((head_count, row_count), jnp.float32),
        jnp.zeros((row_count, head_count, head_size), jnp.float32),
    )
    key_piece = lax.all_gather(keys, "seq", axis=0, tiled=True)
    value_piece = lax.all_gather(values, "seq", axis=0, tiled=True)
    key_count = key_piece.shape[0]
    key_index = jnp.arange(key_count, dtype=jnp.int32) // block_rows
    key_rank = (key_index - oldest) % block_count
    visible = key_rank[None, :] <= query_rank[:, None]

    def update_state(state_old):
        scores = jnp.einsum("qhd,khd->hqk", queries, key_piece, preferred_element_type=jnp.float32)
        weights = jnp.where(visible[None], jnp.exp(scores), 0.0)
        running_sum = jnp.sum(weights, axis=-1)
        weighted = jnp.einsum(
            "hqk,khd->qhd",
            weights.astype(jnp.bfloat16),
            value_piece,
            preferred_element_type=jnp.float32,
        )
        return (running_sum, weighted)

    def keep_state(state_old):
        return state_old

    finished = lax.cond(jnp.any(visible), update_state, keep_state, initial)
    return (finished[1] / finished[0].T[..., None]).astype(jnp.bfloat16)


def local(
    latents, levels, head_slot, fresh_noise, ada_weight, qkv_weight, q_gain, k_gain, out_weight
):
    frames = latents.shape[0]
    seq_devices = lax.axis_size("seq")
    position = lax.axis_index("seq")
    oldest = head_slot[0]
    own_rank = (position - oldest) % seq_devices
    local_terms = modulation_part(levels, ada_weight)
    modulations = lax.all_gather(local_terms, "tensor", axis=1, tiled=True)
    states = latents.astype(jnp.float32)
    hidden = modulate(states, modulations[0][None], modulations[1][None])
    queries, keys, values = project(hidden, qkv_weight, q_gain, k_gain)
    row_rank = jnp.full((frames,), own_rank, jnp.int32)
    attended = attend(queries, row_rank, keys, values, oldest, frames, seq_devices).reshape(
        frames, -1
    )
    partial_sum = jnp.dot(attended, out_weight, preferred_element_type=jnp.float32)
    width_local = fresh_noise.shape[1]
    first_column = lax.axis_index("tensor") * width_local
    projected = lax.psum_scatter(partial_sum, "tensor", scatter_dimension=1, tiled=True)
    own_states = lax.dynamic_slice_in_dim(states, first_column, width_local, 1)
    own_gate = lax.dynamic_slice_in_dim(modulations[2], first_column, width_local, 0)
    updated = (own_states + own_gate[None, :] * projected).astype(jnp.bfloat16)
    leaving_block = spread(updated, "seq", oldest)
    clean_rows = frames // seq_devices
    clean = lax.dynamic_slice_in_dim(leaving_block, position * clean_rows, clean_rows, 0)
    window = jnp.where(own_rank == 0, fresh_noise, updated)
    return (window, clean)


def solution(mesh):
    return jax.shard_map(
        local,
        mesh=mesh,
        in_specs=(
            P("seq", None),
            P("seq"),
            P(),
            P(None, "tensor"),
            P(None, None, "tensor"),
            P(None, None, "tensor"),
            P(),
            P(),
            P("tensor", None),
        ),
        out_specs=(P("seq", "tensor"), P("seq", "tensor")),
        check_vma=False,
    )
```

profile of v0, /device:TPU:1, one launch (start us, length us, event | category | flops | bytes accessed | tf_op | source)
XLA Modules:
  0.0 205.6 jit_solution(5215012281922985482)
XLA Ops:
  8.8 2.3 %copy.14 = bf16[256,3,640]{0,2,1:T(8,128)(2,1)} copy(bf16[256,3,640]{2,0,1:T(8,128)(2,1)} %param.15) | data formatting | bytes 1966080 | tf_op args[4]
  11.1 1.6 fusion.1
  12.7 6.1 %all_gather.9 = f32[3,2560]{1,0:T(4,128)S(1)} all-gather(f32[3,640]{1,0:T(4,128)S(1)} %bitcast.53), channel_id=1, replica_groups=mesh['seq'=8,'tensor'=4] {'tensor'}, dimensions={1}, use_global_device_ids=true | all-gather | bytes 38400 | tf_op jit(solution)/shard_map/all_gather | solution.py:96
  18.8 0.1 fusion.10
  18.8 0.2 convert_reduce_fusion
  19.0 0.3 multiply_reduce_fusion
  19.4 8.9 %copy.15 = bf16[2560,3,384]{0,2,1:T(8,128)(2,1)} copy(bf16[2560,3,384]{2,0,1:T(8,128)(2,1)} %param.16) | data formatting | bytes 11796480 | tf_op args[5]
  28.3 4.5 %fusion.4 = f32[128,3,3,128]{0,3,2,1:T(8,128)S(1)} fusion(bf16[3,3,128,2560]{3,2,1,0:T(8,128)(2,1)} %bitcast.50, bf16[128,2560]{1,0:T(8,128)(2,1)S(1)} %copy-done.1, f32[2560]{0:T(1024)S(1)} %get-tuple-element.30, f32[2560]{0:T(1024)S(1)} %get-tuple-element.29, f32[128]{0:T(128)S(1)} %add_rsqrt_fusion.2, f32[128]{0:T(128)S(1)} %broadcast_multiply_fusion), kind=kOutput, calls=%fused_computation.9 | convolution fusion | flops 756940800 | bytes 7164928 | tf_op jit(solution)/shard_map/dot_general | solution.py:43
  32.9 0.7 multiply_convert_fusion
  33.6 26.9 %all_gather.10 = bf16[1024,3,128]{0,2,1:T(8,128)(2,1)} all-gather(bf16[128,3,128]{0,2,1:T(8,128)(2,1)S(1)} %get-tuple-element.35), channel_id=1, replica_groups=mesh['seq'=8,'tensor'=4] {'seq'}, dimensions={0}, use_global_device_ids=true | all-gather | bytes 884736 | tf_op jit(solution)/shard_map/all_gather | solution.py:61
  60.5 25.2 %all-gather = bf16[1024,1,3,128]{0,3,2,1:T(8,128)(2,1)S(1)} all-gather(bf16[128,1,3,128]{0,3,2,1:T(8,128)(2,1)S(1)} %slice.46), channel_id=2, replica_groups=mesh['seq'=8,'tensor'=4] {'seq'}, dimensions={0}, use_global_device_ids=true | all-gather | bytes 884736 | tf_op jit(solution)/shard_map/all_gather | solution.py:62
  85.8 0.8 broadcast_reduce_fusion
  87.3 4.6 %conditional.1 = (f32[3,128]{1,0:T(4,128)S(1)}, f32[128,3,128]{0,2,1:T(8,128)}) conditional(s32[]{:T(128)} %convert_element_type.40, () %tuple.16, (pred[128,1024]{1,0:T(8,128)(4,1)S(1)}, bf16[128,3,128]{0,2,1:T(8,128)(2,1)}, bf16[1024,3,128]{0,2,1:T(8,128)(2,1)}, bf16[1024,3,128]{0,2,1:T(8,128)(2,1)S(1)}) %tuple.37), branch_computations={%region_5.6_spmd, %region_6.8_spmd} | conditional | flops 202505856 | bytes 3966480 | solution.py:83
  87.3 1.8 fusion.20
  89.1 1.1 convolution_bitcast_fusion
  90.2 1.7 copy.26
  91.9 0.9 divide_convert_fusion
  92.9 1.6 fusion.21
  94.6 1.2 convert_element_type.37
  95.8 29.9 %reduce-scatter.2.cloned.1.call-done = f32[128,640]{1,0:T(8,128)} async-done(((f32[128,2560]{1,0:T(8,128)}), f32[128,640]{1,0:T(8,128)}) %reduce-scatter.2.cloned.1.call-update) | async-done | bytes 327696 | tf_op jit(solution)/shard_map/reduce_scatter | solution.py:107
  125.7 1.8 broadcast_select_fusion
  127.5 0.7 broadcast_select_fusion.1
  128.2 69.2 %all-reduce.2.cloned.1.call-done = bf16[128,640]{1,0:T(8,128)(2,1)} async-done(((bf16[128,640]{1,0:T(8,128)(2,1)}), bf16[128,640]{1,0:T(8,128)(2,1)}) %all-reduce.2.cloned.1.call-update) | async-done | bytes 163856 | tf_op jit(solution)/shard_map/psum | solution.py:11
  197.4 1.3 constant_dynamic-slice_fusion
  (27 shorter events, 0.4 us)
Async XLA Ops:
  7.2 85.7 %copy-start = (bf16[384,2560]{1,0:T(8,128)(2,1)S(1)}, bf16[384,2560]{1,0:T(8,128)(2,1)}, u32[]{:S(2)}) copy-start(bf16[384,2560]{1,0:T(8,128)(2,1)} %param.19) | copy-start | bytes 5898244
  7.2 118.5 %reduce-scatter.2.cloned.1.call-start = ((), (), s32[]{:S(2)}) async-start(), calls=%async_computation.1 | async-start | bytes 1638400 | tf_op jit(solution)/shard_map/reduce_scatter | solution.py:107
  8.8 10.1 %copy-start.1 = (bf16[128,2560]{1,0:T(8,128)(2,1)S(1)}, bf16[128,2560]{1,0:T(8,128)(2,1)}, u32[]{:S(2)}) copy-start(bf16[128,2560]{1,0:T(8,128)(2,1)} %param.11) | copy-start | bytes 1966084
  28.2 4.6 %copy-start.3 = (f32[128]{0:T(128)S(1)}, f32[128]{0:T(128)}, u32[]{:S(2)}) copy-start(f32[128]{0:T(128)} %param.18) | copy-start | bytes 1540
  28.3 4.6 %copy-start.4 = (f32[128]{0:T(128)S(1)}, f32[128]{0:T(128)}, u32[]{:S(2)}) copy-start(f32[128]{0:T(128)} %param.17) | copy-start | bytes 1540
  94.5 33.0 %copy-start.2 = (bf16[128,640]{1,0:T(8,128)(2,1)S(1)}, bf16[128,640]{1,0:T(8,128)(2,1)}, u32[]{:S(2)}) copy-start(bf16[128,640]{1,0:T(8,128)(2,1)} %param.14) | copy-start | bytes 491524
  94.5 102.9 %all-reduce.2.cloned.1.call-start = ((), (), s32[]{:S(2)}) async-start(), calls=%async_computation.2 | async-start | bytes 327680 | tf_op jit(solution)/shard_map/psum | solution.py:11
Sparse Core Ops, SparseCore 0:
  94.6 30.9 reduce-scatter.1
  129.0 68.3 all-reduce.1
where the time goes:
time: 209 us; the launch traced here: 206 us
  waiting for transfers between devices  99.1 us (47%)
  blocking collectives  58.3 us (28%)
  between operations  16.3 us (8%)
  local copies, waits for them, and re-layouts  14.4 us (7%)
  matrix products  10.5 us (5%)
  other arithmetic  6.89 us (3%)
    psum x1, waiting for transfers between devices, spread(): return lax.psum(jnp.where(mine, shard, jnp.zeros_like(shard)), axis)  69.2 us
    reduce_scatter x1, waiting for transfers between devices, local(): lax.psum_scatter(partial_sum, 'tensor', scatter_dimension=1, tiled=True)  29.9 us
    all_gather x1, blocking collectives, attend(): key_piece = lax.all_gather(keys, 'seq', axis=0, tiled=True)  26.9 us
    all_gather x1, blocking collectives, attend(): value_piece = lax.all_gather(values, 'seq', axis=0, tiled=True)  25.2 us
    unnamed x12, local copies, waits for them, and re-layouts  11.3 us
    all_gather x1, blocking collectives, local(): modulations = lax.all_gather(local_terms, 'tensor', axis=1, tiled=True)  6.11 us
    dot_general x1, matrix products, project(): jnp.dot(hidden, qkv_weight.reshape(qkv_weight.shape[0], -1), preferred_el...  4.48 us
  transfers between devices with their start and end apart: 2, of which 2 were waited for; matrix products, arithmetic and copies ran while one was open for 1% of the time, Pallas kernels for 0%

commit v1 on v0

v1 whole, which is shorter than its diff:
```python
import functools
import math

import jax
import jax.numpy as jnp
from jax import lax
from jax.experimental import pallas as pl
from jax.experimental.pallas import tpu as pltpu
from jax.sharding import PartitionSpec as P

F32 = jnp.float32
BF16 = jnp.bfloat16
EPS = 1e-06


def embed(levels, width):
    half_width = width // 2
    frequency = jnp.exp(-math.log(10000.0) * jnp.arange(half_width, dtype=F32) / half_width)
    angles = levels.astype(F32)[:, None] * frequency[None, :]
    return jax.nn.silu(jnp.concatenate([jnp.cos(angles), jnp.sin(angles)], axis=1)).astype(BF16)


def dot(a, b):
    return jnp.dot(a, b, preferred_element_type=F32)


def dot_t(a, b):
    return lax.dot_general(a, b, (((1,), (1,)), ((), ())), preferred_element_type=F32)


def kernel(
    n, parts, slab, clean_rows,
    head_ref, emb_ref, gains_ref, lat_hbm, noise_ref, ada_hbm, qkv_hbm, out_hbm,
    window_ref, clean_ref,
    lat, ada, wqkv, wout, normed, hidden, mods, gates, lat_rows, kv, queries, q_rows,
    acc, totals, attended, sums_out, sums_in, own_sum,
    load_sem, mod_send, mod_recv, gate_send, gate_recv, row_send, row_recv,
    kv_send, kv_recv, q_send, q_recv, sum_send, sum_recv,
):
    me = lax.axis_index("seq")
    part = lax.axis_index("tensor")
    rows, width = lat.shape
    columns = window_ref.shape[1]
    head_size = gains_ref.shape[1]
    heads = queries.shape[1] // head_size

    def remote(src, dst, send, recv, axis, target):
        return pltpu.make_async_remote_copy(
            src_ref=src, dst_ref=dst, send_sem=send, recv_sem=recv,
            device_id={axis: target}, device_id_type=pl.DeviceIdType.MESH,
        )

    loads = [
        pltpu.make_async_copy(ada_hbm, ada, load_sem.at[0]),
        pltpu.make_async_copy(lat_hbm, lat, load_sem.at[1]),
        pltpu.make_async_copy(qkv_hbm.at[1], wqkv.at[1], load_sem.at[2]),
        pltpu.make_async_copy(qkv_hbm.at[2], wqkv.at[2], load_sem.at[3]),
        pltpu.make_async_copy(qkv_hbm.at[0], wqkv.at[0], load_sem.at[4]),
        pltpu.make_async_copy(out_hbm, wout, load_sem.at[5]),
    ]
    for load in loads:
        load.start()

    barrier = pltpu.get_barrier_semaphore()
    for step in range(1, parts):
        pl.semaphore_signal(
            barrier, inc=1, device_id={"tensor": lax.rem(part + step, parts)},
            device_id_type=pl.DeviceIdType.MESH,
        )

    @pl.loop(1, n)
    def _(step):
        pl.semaphore_signal(
            barrier, inc=1, device_id={"seq": lax.rem(me + step, n)},
            device_id_type=pl.DeviceIdType.MESH,
        )

    loads[0].wait()
    emb = jnp.broadcast_to(emb_ref[...], (16, emb_ref.shape[1]))
    terms = [dot(emb, ada[j])[0:1] for j in range(3)]
    mine = jnp.concatenate(terms + [jnp.zeros((5, columns), F32)], axis=0)
    mods[part] = mine
    gates[me] = mine

    pl.semaphore_wait(barrier, n - 1 + parts - 1)

    def mod_copy(slot, target):
        return remote(
            mods.at[slot], mods.at[slot], mod_send.at[target], mod_recv.at[slot], "tensor", target
        )

    for step in range(1, parts):
        mod_copy(part, lax.rem(part + step, parts)).start()

    loads[1].wait()

    def slab_of(device):
        return pl.multiple_of((device * clean_rows) // slab * slab, slab)

    first_column = pl.multiple_of(part * columns, 128)

    def gate_copy(slot, target):
        return remote(
            gates.at[slot], gates.at[slot], gate_send.at[target], gate_recv.at[slot], "seq", target
        )

    def row_copy(slot, target):
        return remote(
            lat.at[pl.ds(slab_of(target), slab), pl.ds(first_column, columns)],
            lat_rows.at[slot], row_send.at[target], row_recv.at[slot], "seq", target,
        )

    own_slab = slab_of(me)
    lat_rows[me] = lat[pl.ds(own_slab, slab), pl.ds(first_column, columns)]

    tile = 16

    @pl.loop(0, rows // tile)
    def _(index):
        at = pl.ds(pl.multiple_of(index * tile, tile), tile)
        states = lat[at, :].astype(F32)
        centered = states - jnp.mean(states, axis=-1, keepdims=True)
        variance = jnp.mean(centered * centered, axis=-1, keepdims=True)
        normed[at, :] = centered * lax.rsqrt(variance + EPS)

    for step in range(1, parts):
        mod_copy(lax.rem(part + step, parts), part).wait_recv()
    for index in range(parts):
        at = slice(index * columns, (index + 1) * columns)
        hidden[:, at] = (
            normed[:, at] * (1.0 + mods[index, 1:2, :]) + mods[index, 0:1, :]
        ).astype(BF16)

    def scaled(matrix, gain, factor):
        power = jnp.mean(matrix * matrix, axis=-1, keepdims=True)
        return (matrix * lax.rsqrt(power + EPS) * gain * factor).astype(BF16)

    def kv_copy(kind, slot, target):
        return remote(
            kv.at[slot, kind], kv.at[slot, kind],
            kv_send.at[kind, target], kv_recv.at[kind, slot], "seq", target,
        )

    def q_copy(slot, target):
        return remote(
            queries.at[pl.ds(slab_of(target), slab), :], q_rows.at[slot],
            q_send.at[target], q_recv.at[slot], "seq", target,
        )

    def head_at(index):
        return slice(index * head_size, (index + 1) * head_size)

    loads[2].wait()
    raw = dot(hidden[...], wqkv[1])
    for h in range(heads):
        kv[me, 0, :, head_at(h)] = scaled(raw[:, head_at(h)], gains_ref[1:2, :], 1.0)

    @pl.loop(1, n)
    def _(step):
        kv_copy(0, me, lax.rem(me + step, n)).start()

    loads[3].wait()
    kv[me, 1] = dot(hidden[...], wqkv[2]).astype(BF16)

    @pl.loop(1, n)
    def _(step):
        kv_copy(1, me, lax.rem(me + step, n)).start()

    loads[4].wait()
    raw = dot(hidden[...], wqkv[0])
    for h in range(heads):
        queries[:, head_at(h)] = scaled(
            raw[:, head_at(h)], gains_ref[0:1, :], 1.0 / math.sqrt(head_size)
        )
    q_rows[me] = queries[pl.ds(own_slab, slab), :]

    @pl.loop(1, n)
    def _(step):
        target = lax.rem(me + step, n)
        q_copy(me, target).start()
        gate_copy(me, target).start()
        row_copy(me, target).start()

    oldest = head_ref[0]
    own_rank = lax.rem(me - oldest + n, n)

    for h in range(heads):
        weights = jnp.exp(dot_t(queries[:, head_at(h)], kv[me, 0, :, head_at(h)]))
        totals[:, head_at(h)] = weights
        acc[:, head_at(h)] = dot(weights.astype(BF16), kv[me, 1, :, head_at(h)])

    @pl.loop(1, n)
    def _(step):
        source = lax.rem(me - step + n, n)
        kv_copy(0, source, me).wait_recv()
        kv_copy(1, source, me).wait_recv()
        rank = lax.rem(source - oldest + n, n)
        seen = jnp.full((rows, rows), rank, jnp.int32) <= own_rank
        for h in range(heads):
            scores = dot_t(queries[:, head_at(h)], kv[source, 0, :, head_at(h)])
            weights = jnp.where(seen, jnp.exp(scores), 0.0)
            totals[:, head_at(h)] += weights
            acc[:, head_at(h)] += dot(weights.astype(BF16), kv[source, 1, :, head_at(h)])

    @pl.loop(1, n)
    def _(step):
        source = lax.rem(me - step + n, n)
        q_copy(source, me).wait_recv()
        gate_copy(source, me).wait_recv()
        row_copy(source, me).wait_recv()

    for h in range(heads):
        total = jnp.sum(totals[:, head_at(h)], axis=-1, keepdims=True)
        attended[0:rows, head_at(h)] = (acc[:, head_at(h)] / total).astype(BF16)
        weights = jnp.exp(dot_t(q_rows[oldest, :, head_at(h)], kv[oldest, 0, :, head_at(h)]))
        total = jnp.sum(weights, axis=-1, keepdims=True)
        product = dot(weights.astype(BF16), kv[oldest, 1, :, head_at(h)])
        attended[rows:, head_at(h)] = (product / total).astype(BF16)

    def sum_copy(slot, target):
        return remote(
            sums_out.at[target], sums_in.at[slot], sum_send.at[target], sum_recv.at[slot],
            "tensor", target,
        )

    loads[5].wait()
    for step in range(1, parts):
        target = lax.rem(part + step, parts)
        at = pl.ds(pl.multiple_of(target * columns, 128), columns)
        sums_out[target] = dot(attended[...], wout[:, at]).astype(BF16)
        sum_copy(part, target).start()
    own_sum[...] = dot(attended[...], wout[:, pl.ds(first_column, columns)])
    for step in range(1, parts):
        sum_copy(lax.rem(part + step, parts), part).wait_recv()

    total = own_sum[...]
    for step in range(1, parts):
        total += sums_in[lax.rem(part + step, parts)].astype(F32)
    own_states = lat[:, pl.ds(first_column, columns)].astype(F32)
    updated = (own_states + gates[me, 2:3, :] * total[0:rows]).astype(BF16)
    leaving = jnp.full((rows, columns), own_rank, jnp.int32) == 0
    window_ref[...] = jnp.where(leaving, noise_ref[...], updated)
    clean_ref[...] = (
        lat_rows[oldest].astype(F32) + gates[oldest, 2:3, :] * total[rows:]
    ).astype(BF16)

    for step in range(1, parts):
        target = lax.rem(part + step, parts)
        mod_copy(part, target).wait_send()
        sum_copy(part, target).wait_send()

    @pl.loop(1, n)
    def _(step):
        target = lax.rem(me + step, n)
        kv_copy(0, me, target).wait_send()
        kv_copy(1, me, target).wait_send()
        q_copy(me, target).wait_send()
        gate_copy(me, target).wait_send()
        row_copy(me, target).wait_send()


def local(
    latents, levels, head_slot, fresh_noise, ada_weight, qkv_weight, q_gain, k_gain, out_weight
):
    n = lax.axis_size("seq")
    parts = lax.axis_size("tensor")
    rows, width = latents.shape
    columns = fresh_noise.shape[1]
    inner = out_weight.shape[0]
    clean_rows = rows // n
    slab = max(clean_rows, 16)
    embedding = embed(levels, ada_weight.shape[0])
    gains = jnp.stack([q_gain, k_gain])
    vmem = pl.BlockSpec(memory_space=pltpu.VMEM)
    hbm = pl.BlockSpec(memory_space=pl.ANY)
    dma = pltpu.SemaphoreType.DMA
    window, clean = pl.pallas_call(
        functools.partial(kernel, n, parts, slab, clean_rows),
        out_shape=(
            jax.ShapeDtypeStruct((rows, columns), BF16),
            jax.ShapeDtypeStruct((slab, columns), BF16),
        ),
        in_specs=[
            pl.BlockSpec(memory_space=pltpu.SMEM), vmem, vmem, hbm, vmem, hbm, hbm, hbm,
        ],
        out_specs=(vmem, vmem),
        scratch_shapes=[
            pltpu.VMEM((rows, width), BF16),
            pltpu.VMEM((3, ada_weight.shape[0], columns), BF16),
            pltpu.VMEM((3, width, inner), BF16),
            pltpu.VMEM((inner, width), BF16),
            pltpu.VMEM((rows, width), F32),
            pltpu.VMEM((rows, width), BF16),
            pltpu.VMEM((parts, 8, columns), F32),
            pltpu.VMEM((n, 8, columns), F32),
            pltpu.VMEM((n, slab, columns), BF16),
            pltpu.VMEM((n, 2, rows, inner), BF16),
            pltpu.VMEM((rows, inner), BF16),
            pltpu.VMEM((n, slab, inner), BF16),
            pltpu.VMEM((rows, inner), F32),
            pltpu.VMEM((rows, inner), F32),
            pltpu.VMEM((rows + slab, inner), BF16),
            pltpu.VMEM((parts, rows + slab, columns), BF16),
            pltpu.VMEM((parts, rows + slab, columns), BF16),
            pltpu.VMEM((rows + slab, columns), F32),
            dma((6,)), dma((parts,)), dma((parts,)), dma((n,)), dma((n,)), dma((n,)), dma((n,)),
            dma((2, n)), dma((2, n)), dma((n,)), dma((n,)), dma((parts,)), dma((parts,)),
        ],
        compiler_params=pltpu.CompilerParams(
            collective_id=0, has_side_effects=True, vmem_limit_bytes=60 * 1024 * 1024
        ),
    )(
        head_slot, embedding, gains, latents, fresh_noise,
        jnp.transpose(ada_weight, (1, 0, 2)), jnp.transpose(qkv_weight, (1, 0, 2)), out_weight,
    )
    if clean_rows < slab:
        start = (lax.axis_index("seq") * clean_rows) % slab
        clean = lax.dynamic_slice_in_dim(clean, start, clean_rows, 0)
    return window, clean


def solution(mesh):
    return jax.shard_map(
        local,
        mesh=mesh,
        in_specs=(
            P("seq", None),
            P("seq"),
            P(),
            P(None, "tensor"),
            P(None, None, "tensor"),
            P(None, None, "tensor"),
            P(),
            P(),
            P("tensor", None),
        ),
        out_specs=(P("seq", "tensor"), P("seq", "tensor")),
        check_vma=False,
    )
```

time: 209 us -> 71.9 us (0.34)
  the two profiles are of different devices: /device:TPU:1 before, /device:TPU:11 now
where the time goes in v1:
time: 71.9 us; the launch traced here: 71.7 us
  Pallas kernels  64.9 us (90%)
  local copies, waits for them, and re-layouts  2.93 us (4%)
  between operations  1.94 us (3%)
  other arithmetic  1.88 us (3%)
    pallas_call x1, Pallas kernels, local(): pl.pallas_call(functools.partial(kernel, n, parts, slab, clean_rows), out...  64.9 us
    unnamed x2, local copies, waits for them, and re-layouts  2.93 us

profile of v1, /device:TPU:11, one launch (start us, length us, event | category | flops | bytes accessed | tf_op | source)
XLA Modules:
  0.0 71.7 jit_solution(16871930707102507497)
XLA Ops:
  2.0 0.6 fusion.emb_ref
  2.6 1.2 %pad_maximum_fusion.1.gains_ref = f32[2,128]{1,0:T(2,128)} fusion(f32[1,128]{1,0:T(1,128)} %bitcast.11, f32[1,128]{1,0:T(1,128)} %bitcast.12), kind=kLoop, calls=%fused_computation.2 | loop fusion | flops 256 | bytes 2048 | tf_op jit(solution)/shard_map/stack | solution.py:273
  3.8 64.9 %shard_map.104 = (bf16[128,640]{1,0:T(8,128)(2,1)}, bf16[16,640]{1,0:T(8,128)(2,1)}) custom-call(s32[1]{0:T(128)S(6)} %copy.14.head_ref, bf16[1,256]{1,0:T(2,128)(2,1)} %fusion.emb_ref, f32[2,128]{1,0:T(2,128)} %pad_maximum_fusion.1.gains_ref, bf16[128,2560]{1,0:T(8,128)(2,1)} %lat_hbm.1, bf16[128,640]{1,0:T(8,128)(2,1)} %noise_ref.1, ...), custom_call_target="tpu_custom_call" | custom-call | tf_op jit(solution)/shard_map/pallas_call | solution.py:277
  68.8 1.6 %copy.15 = bf16[128,640]{1,0:T(8,128)(2,1)} copy(bf16[128,640]{1,0:T(8,128)(2,1)} %get-tuple-element.6) | data formatting | bytes 327680
  70.4 1.3 %copy.16 = bf16[16,640]{1,0:T(8,128)(2,1)} copy(bf16[16,640]{1,0:T(8,128)(2,1)} %get-tuple-element.7) | data formatting | bytes 40960
  (1 shorter events, 0.0 us)

commit v2 on v1

--- a/solution.py
+++ b/solution.py
@@ -39,6 +39,8 @@
 ):
     me = lax.axis_index("seq")
     part = lax.axis_index("tensor")
+    pair = 2
+    side = lax.rem(me, pair)
     rows, width = lat.shape
     columns = window_ref.shape[1]
     head_size = gains_ref.shape[1]
@@ -135,11 +137,30 @@
         power = jnp.mean(matrix * matrix, axis=-1, keepdims=True)
         return (matrix * lax.rsqrt(power + EPS) * gain * factor).astype(BF16)
 
-    def kv_copy(kind, slot, target):
+    def kv_copy(kind, slot, way, target):
         return remote(
             kv.at[slot, kind], kv.at[slot, kind],
-            kv_send.at[kind, target], kv_recv.at[kind, slot], "seq", target,
-        )
+            kv_send.at[kind, way, slot], kv_recv.at[kind, slot], "seq", target,
+        )
+
+    def onward(kind, slot, way, act):
+        target = (me - pair, me + pair, me + 1 - 2 * side)[way]
+        there = (target >= 0, target < n, None)[way]
+        run = functools.partial(act, kind, slot, way, target)
+        if there is None:
+            run()
+        else:
+            pl.when(there)(run)
+
+    def start(kind, slot, way, target):
+        kv_copy(kind, slot, way, target).start()
+
+    def finish(kind, slot, way, target):
+        kv_copy(kind, slot, way, target).wait_send()
+
+    def spread_out(kind, slot):
+        for way in range(3):
+            onward(kind, slot, way, start)
 
     def q_copy(slot, target):
         return remote(
@@ -155,16 +176,12 @@
     for h in range(heads):
         kv[me, 0, :, head_at(h)] = scaled(raw[:, head_at(h)], gains_ref[1:2, :], 1.0)
 
-    @pl.loop(1, n)
-    def _(step):
-        kv_copy(0, me, lax.rem(me + step, n)).start()
+    spread_out(0, me)
 
     loads[3].wait()
     kv[me, 1] = dot(hidden[...], wqkv[2]).astype(BF16)
 
-    @pl.loop(1, n)
-    def _(step):
-        kv_copy(1, me, lax.rem(me + step, n)).start()
+    spread_out(1, me)
 
     loads[4].wait()
     raw = dot(hidden[...], wqkv[0])
@@ -189,11 +206,7 @@
         totals[:, head_at(h)] = weights
         acc[:, head_at(h)] = dot(weights.astype(BF16), kv[me, 1, :, head_at(h)])
 
-    @pl.loop(1, n)
-    def _(step):
-        source = lax.rem(me - step + n, n)
-        kv_copy(0, source, me).wait_recv()
-        kv_copy(1, source, me).wait_recv()
+    def absorb(source):
         rank = lax.rem(source - oldest + n, n)
         seen = jnp.full((rows, rows), rank, jnp.int32) <= own_rank
         for h in range(heads):
@@ -201,6 +214,60 @@
             weights = jnp.where(seen, jnp.exp(scores), 0.0)
             totals[:, head_at(h)] += weights
             acc[:, head_at(h)] += dot(weights.astype(BF16), kv[source, 1, :, head_at(h)])
+
+    def take_across(source):
+        kv_copy(0, source, 2, me).wait_recv()
+        kv_copy(1, source, 2, me).wait_recv()
+        absorb(source)
+
+    other = me + 1 - 2 * side
+
+    @pl.loop(1, n // pair)
+    def _(step):
+        below, above = me - step * pair, me + step * pair
+        for kind in range(2):
+
+            @pl.when(below >= 0)
+            def _():
+                kv_copy(kind, below, 1, me).wait_recv()
+                onward(kind, below, 1, start)
+                onward(kind, below, 2, start)
+
+            @pl.when(above < n)
+            def _():
+                kv_copy(kind, above, 0, me).wait_recv()
+                onward(kind, above, 0, start)
+                onward(kind, above, 2, start)
+
+        @pl.when(step == 1)
+        def _():
+            take_across(other)
+
+        @pl.when((step > 1) & (other - (step - 1) * pair >= 0))
+        def _():
+            take_across(other - (step - 1) * pair)
+
+        @pl.when((step > 1) & (other + (step - 1) * pair < n))
+        def _():
+            take_across(other + (step - 1) * pair)
+
+        @pl.when(below >= 0)
+        def _():
+            absorb(below)
+
+        @pl.when(above < n)
+        def _():
+            absorb(above)
+
+    last = n - pair
+
+    @pl.when(other - last >= 0)
+    def _():
+        take_across(other - last)
+
+    @pl.when(other + last < n)
+    def _():
+        take_across(other + last)
 
     @pl.loop(1, n)
     def _(step):
@@ -252,11 +319,28 @@
     @pl.loop(1, n)
     def _(step):
         target = lax.rem(me + step, n)
-        kv_copy(0, me, target).wait_send()
-        kv_copy(1, me, target).wait_send()
         q_copy(me, target).wait_send()
         gate_copy(me, target).wait_send()
         row_copy(me, target).wait_send()
+
+    for kind in range(2):
+        for way in range(3):
+            onward(kind, me, way, finish)
+
+    @pl.loop(1, n // pair)
+    def _(step):
+        below, above = me - step * pair, me + step * pair
+        for kind in range(2):
+
+            @pl.when(below >= 0)
+            def _():
+                onward(kind, below, 1, finish)
+                onward(kind, below, 2, finish)
+
+            @pl.when(above < n)
+            def _():
+                onward(kind, above, 0, finish)
+                onward(kind, above, 2, finish)
 
 
 def local(
@@ -304,7 +388,7 @@
             pltpu.VMEM((parts, rows + slab, columns), BF16),
             pltpu.VMEM((rows + slab, columns), F32),
             dma((6,)), dma((parts,)), dma((parts,)), dma((n,)), dma((n,)), dma((n,)), dma((n,)),
-            dma((2, n)), dma((2, n)), dma((n,)), dma((n,)), dma((parts,)), dma((parts,)),
+            dma((2, 3, n)), dma((2, n)), dma((n,)), dma((n,)), dma((parts,)), dma((parts,)),
         ],
         compiler_params=pltpu.CompilerParams(
             collective_id=0, has_side_effects=True, vmem_limit_bytes=60 * 1024 * 1024

time: 71.9 us -> 56.2 us (0.78)
  the two profiles are of different devices: /device:TPU:11 before, /device:TPU:1 now
where the time goes in v2:
time: 56.2 us; the launch traced here: 55.9 us
  Pallas kernels  49.2 us (88%)
  local copies, waits for them, and re-layouts  2.93 us (5%)
  between operations  1.94 us (3%)
  other arithmetic  1.88 us (3%)
    pallas_call x1, Pallas kernels, local(): pl.pallas_call(functools.partial(kernel, n, parts, slab, clean_rows), out...  49.2 us
    unnamed x2, local copies, waits for them, and re-layouts  2.93 us
    another operation x1, other arithmetic, local(): gains = jnp.stack([q_gain, k_gain])  1.24 us

profile of v2, /device:TPU:1, one launch (start us, length us, event | category | flops | bytes accessed | tf_op | source)
XLA Modules:
  0.0 55.9 jit_solution(3160333896429085783)
XLA Ops:
  2.0 0.6 %fusion.emb_ref = bf16[1,256]{1,0:T(2,128)(2,1)} fusion(f32[1,128]{1,0:T(1,128)S(1)} %get-tuple-element.2, f32[1,128]{1,0:T(1,128)S(1)} %get-tuple-element.3), kind=kLoop, calls=%fused_computation.3 | loop fusion | flops 1536 | bytes 1536 | tf_op jit(solution)/shard_map/convert_element_type | solution.py:20
  2.6 1.2 %pad_maximum_fusion.1.gains_ref = f32[2,128]{1,0:T(2,128)} fusion(f32[1,128]{1,0:T(1,128)} %bitcast.11, f32[1,128]{1,0:T(1,128)} %bitcast.12), kind=kLoop, calls=%fused_computation.2 | loop fusion | flops 256 | bytes 2048 | tf_op jit(solution)/shard_map/stack | solution.py:357
  3.8 49.2 %shard_map.104 = (bf16[128,640]{1,0:T(8,128)(2,1)}, bf16[16,640]{1,0:T(8,128)(2,1)}) custom-call(s32[1]{0:T(128)S(6)} %copy.14.head_ref, bf16[1,256]{1,0:T(2,128)(2,1)} %fusion.emb_ref, f32[2,128]{1,0:T(2,128)} %pad_maximum_fusion.1.gains_ref, bf16[128,2560]{1,0:T(8,128)(2,1)} %lat_hbm.1, bf16[128,640]{1,0:T(8,128)(2,1)} %noise_ref.1, ...), custom_call_target="tpu_custom_call" | custom-call | tf_op jit(solution)/shard_map/pallas_call | solution.py:361
  53.0 1.6 %copy.15 = bf16[128,640]{1,0:T(8,128)(2,1)} copy(bf16[128,640]{1,0:T(8,128)(2,1)} %get-tuple-element.6) | data formatting | bytes 327680
  54.6 1.3 %copy.16 = bf16[16,640]{1,0:T(8,128)(2,1)} copy(bf16[16,640]{1,0:T(8,128)(2,1)} %get-tuple-element.7) | data formatting | bytes 40960
  (1 shorter events, 0.0 us)

commit v3 on v2

--- a/solution.py
+++ b/solution.py
@@ -13,13 +13,6 @@
 EPS = 1e-06
 
 
-def embed(levels, width):
-    half_width = width // 2
-    frequency = jnp.exp(-math.log(10000.0) * jnp.arange(half_width, dtype=F32) / half_width)
-    angles = levels.astype(F32)[:, None] * frequency[None, :]
-    return jax.nn.silu(jnp.concatenate([jnp.cos(angles), jnp.sin(angles)], axis=1)).astype(BF16)
-
-
 def dot(a, b):
     return jnp.dot(a, b, preferred_element_type=F32)
 
@@ -30,20 +23,20 @@
 
 def kernel(
     n, parts, slab, clean_rows,
-    head_ref, emb_ref, gains_ref, lat_hbm, noise_ref, ada_hbm, qkv_hbm, out_hbm,
-    window_ref, clean_ref,
+    head_ref, level_ref, q_gain_ref, k_gain_ref, lat_hbm, ada_hbm, qkv_hbm, out_hbm,
+    updated_ref,
     lat, ada, wqkv, wout, normed, hidden, mods, gates, lat_rows, kv, queries, q_rows,
-    acc, totals, attended, sums_out, sums_in, own_sum,
+    acc, totals, attended,
     load_sem, mod_send, mod_recv, gate_send, gate_recv, row_send, row_recv,
-    kv_send, kv_recv, q_send, q_recv, sum_send, sum_recv,
+    kv_send, kv_recv, q_send, q_recv, w_send, w_recv, att_send, att_recv,
 ):
     me = lax.axis_index("seq")
     part = lax.axis_index("tensor")
     pair = 2
     side = lax.rem(me, pair)
     rows, width = lat.shape
-    columns = window_ref.shape[1]
-    head_size = gains_ref.shape[1]
+    columns = updated_ref.shape[1]
+    head_size = q_gain_ref.shape[1]
     heads = queries.shape[1] // head_size
 
     def remote(src, dst, send, recv, axis, target):
@@ -58,7 +51,10 @@
         pltpu.make_async_copy(qkv_hbm.at[1], wqkv.at[1], load_sem.at[2]),
         pltpu.make_async_copy(qkv_hbm.at[2], wqkv.at[2], load_sem.at[3]),
         pltpu.make_async_copy(qkv_hbm.at[0], wqkv.at[0], load_sem.at[4]),
-        pltpu.make_async_copy(out_hbm, wout, load_sem.at[5]),
+        pltpu.make_async_copy(
+            out_hbm.at[:, pl.ds(pl.multiple_of(part * columns, 128), columns)],
+            wout.at[part], load_sem.at[5],
+        ),
     ]
     for load in loads:
         load.start()
@@ -77,12 +73,15 @@
             device_id_type=pl.DeviceIdType.MESH,
         )
 
+    half_width = ada.shape[1] // 2
+    order = lax.broadcasted_iota(jnp.int32, (16, half_width), 1).astype(F32)
+    angles = level_ref[0].astype(F32) * jnp.exp(-math.log(10000.0) * order / half_width)
+    waves = jnp.concatenate([jnp.cos(angles), jnp.sin(angles)], axis=1)
+    emb = (waves * (1.0 / (1.0 + jnp.exp(-waves)))).astype(BF16)
     loads[0].wait()
-    emb = jnp.broadcast_to(emb_ref[...], (16, emb_ref.shape[1]))
-    terms = [dot(emb, ada[j])[0:1] for j in range(3)]
-    mine = jnp.concatenate(terms + [jnp.zeros((5, columns), F32)], axis=0)
-    mods[part] = mine
-    gates[me] = mine
+    for j in range(2):
+        mods[part, j : j + 1, :] = dot(emb, ada[j])[0:1]
+    gates[me] = dot(emb, ada[2])[0:1]
 
     pl.semaphore_wait(barrier, n - 1 + parts - 1)
 
@@ -94,7 +93,6 @@
     for step in range(1, parts):
         mod_copy(part, lax.rem(part + step, parts)).start()
 
-    loads[1].wait()
 
     def slab_of(device):
         return pl.multiple_of((device * clean_rows) // slab * slab, slab)
@@ -108,10 +106,26 @@
 
     def row_copy(slot, target):
         return remote(
-            lat.at[pl.ds(slab_of(target), slab), pl.ds(first_column, columns)],
+            lat_hbm.at[pl.ds(slab_of(target), slab), pl.ds(first_column, columns)],
             lat_rows.at[slot], row_send.at[target], row_recv.at[slot], "seq", target,
         )
 
+    def w_copy(slot, target):
+        at = pl.ds(pl.multiple_of(target * columns, 128), columns)
+        return remote(
+            out_hbm.at[:, at], wout.at[slot], w_send.at[target], w_recv.at[slot], "tensor", target
+        )
+
+    @pl.loop(1, n)
+    def _(step):
+        target = lax.rem(me + step, n)
+        gate_copy(me, target).start()
+        row_copy(me, target).start()
+
+    for step in range(1, parts):
+        w_copy(part, lax.rem(part + step, parts)).start()
+
+    loads[1].wait()
     own_slab = slab_of(me)
     lat_rows[me] = lat[pl.ds(own_slab, slab), pl.ds(first_column, columns)]
 
@@ -174,7 +188,7 @@
     loads[2].wait()
     raw = dot(hidden[...], wqkv[1])
     for h in range(heads):
-        kv[me, 0, :, head_at(h)] = scaled(raw[:, head_at(h)], gains_ref[1:2, :], 1.0)
+        kv[me, 0, :, head_at(h)] = scaled(raw[:, head_at(h)], k_gain_ref[...], 1.0)
 
     spread_out(0, me)
 
@@ -187,7 +201,7 @@
     raw = dot(hidden[...], wqkv[0])
     for h in range(heads):
         queries[:, head_at(h)] = scaled(
-            raw[:, head_at(h)], gains_ref[0:1, :], 1.0 / math.sqrt(head_size)
+            raw[:, head_at(h)], q_gain_ref[...], 1.0 / math.sqrt(head_size)
         )
     q_rows[me] = queries[pl.ds(own_slab, slab), :]
 
@@ -195,8 +209,6 @@
     def _(step):
         target = lax.rem(me + step, n)
         q_copy(me, target).start()
-        gate_copy(me, target).start()
-        row_copy(me, target).start()
 
     oldest = head_ref[0]
     own_rank = lax.rem(me - oldest + n, n)
@@ -278,43 +290,56 @@
 
     for h in range(heads):
         total = jnp.sum(totals[:, head_at(h)], axis=-1, keepdims=True)
-        attended[0:rows, head_at(h)] = (acc[:, head_at(h)] / total).astype(BF16)
+        attended[part, 0:rows, head_at(h)] = (acc[:, head_at(h)] / total).astype(BF16)
         weights = jnp.exp(dot_t(q_rows[oldest, :, head_at(h)], kv[oldest, 0, :, head_at(h)]))
         total = jnp.sum(weights, axis=-1, keepdims=True)
         product = dot(weights.astype(BF16), kv[oldest, 1, :, head_at(h)])
-        attended[rows:, head_at(h)] = (product / total).astype(BF16)
-
-    def sum_copy(slot, target):
-        return remote(
-            sums_out.at[target], sums_in.at[slot], sum_send.at[target], sum_recv.at[slot],
+        attended[part, rows:, head_at(h)] = (product / total).astype(BF16)
+
+    core = lax.rem(part, 2)
+    sibling = part + 1 - 2 * core
+
+    def att_copy(slot, target, way):
+        return remote(
+            attended.at[slot], attended.at[slot], att_send.at[way], att_recv.at[slot],
             "tensor", target,
         )
 
+    ahead = [lax.rem(part + 2 * step, parts) for step in range(1, parts // 2)]
+    for way, target in enumerate(ahead):
+        att_copy(part, target, way).start()
+    att_copy(part, sibling, len(ahead)).start()
+
     loads[5].wait()
-    for step in range(1, parts):
-        target = lax.rem(part + step, parts)
-        at = pl.ds(pl.multiple_of(target * columns, 128), columns)
-        sums_out[target] = dot(attended[...], wout[:, at]).astype(BF16)
-        sum_copy(part, target).start()
-    own_sum[...] = dot(attended[...], wout[:, pl.ds(first_column, columns)])
-    for step in range(1, parts):
-        sum_copy(lax.rem(part + step, parts), part).wait_recv()
-
-    total = own_sum[...]
-    for step in range(1, parts):
-        total += sums_in[lax.rem(part + step, parts)].astype(F32)
+    total = dot(attended[part], wout[part])
+
+    def add(slot, total):
+        w_copy(slot, part).wait_recv()
+        return total + dot(attended[slot], wout[slot])
+
+    att_copy(sibling, part, 0).wait_recv()
+    total = add(sibling, total)
+    for way, slot in enumerate(ahead):
+        att_copy(slot, part, 0).wait_recv()
+        att_copy(slot, sibling, len(ahead) + 1 + way).start()
+        total = add(slot, total)
+    for slot in ahead:
+        handed = slot + 1 - 2 * core
+        att_copy(handed, part, 0).wait_recv()
+        total = add(handed, total)
+
     own_states = lat[:, pl.ds(first_column, columns)].astype(F32)
-    updated = (own_states + gates[me, 2:3, :] * total[0:rows]).astype(BF16)
-    leaving = jnp.full((rows, columns), own_rank, jnp.int32) == 0
-    window_ref[...] = jnp.where(leaving, noise_ref[...], updated)
-    clean_ref[...] = (
-        lat_rows[oldest].astype(F32) + gates[oldest, 2:3, :] * total[rows:]
+    updated_ref[0:rows, :] = (own_states + gates[me] * total[0:rows]).astype(BF16)
+    updated_ref[rows:, :] = (
+        lat_rows[oldest].astype(F32) + gates[oldest] * total[rows:]
     ).astype(BF16)
 
+    for way in range(parts - 1):
+        att_copy(part, sibling, way).wait_send()
     for step in range(1, parts):
         target = lax.rem(part + step, parts)
         mod_copy(part, target).wait_send()
-        sum_copy(part, target).wait_send()
+        w_copy(part, target).wait_send()
 
     @pl.loop(1, n)
     def _(step):
@@ -341,6 +366,14 @@
             def _():
                 onward(kind, above, 0, finish)
                 onward(kind, above, 2, finish)
+
+
+def finish_kernel(n, head_ref, updated_ref, noise_ref, window_ref, clean_ref):
+    rows = window_ref.shape[0]
+    own_rank = lax.rem(lax.axis_index("seq") - head_ref[0] + n, n)
+    leaving = jnp.full(window_ref.shape, own_rank, jnp.int32) == 0
+    window_ref[...] = jnp.where(leaving, noise_ref[...], updated_ref[0:rows, :])
+    clean_ref[...] = updated_ref[rows:, :]
 
 
 def local(
@@ -353,50 +386,53 @@
     inner = out_weight.shape[0]
     clean_rows = rows // n
     slab = max(clean_rows, 16)
-    embedding = embed(levels, ada_weight.shape[0])
-    gains = jnp.stack([q_gain, k_gain])
     vmem = pl.BlockSpec(memory_space=pltpu.VMEM)
+    smem = pl.BlockSpec(memory_space=pltpu.SMEM)
     hbm = pl.BlockSpec(memory_space=pl.ANY)
     dma = pltpu.SemaphoreType.DMA
-    window, clean = pl.pallas_call(
+    updated = pl.pallas_call(
         functools.partial(kernel, n, parts, slab, clean_rows),
-        out_shape=(
-            jax.ShapeDtypeStruct((rows, columns), BF16),
-            jax.ShapeDtypeStruct((slab, columns), BF16),
-        ),
+        out_shape=jax.ShapeDtypeStruct((rows + slab, columns), BF16),
         in_specs=[
-            pl.BlockSpec(memory_space=pltpu.SMEM), vmem, vmem, hbm, vmem, hbm, hbm, hbm,
+            smem, smem, vmem, vmem, hbm, hbm, hbm, hbm,
         ],
-        out_specs=(vmem, vmem),
+        out_specs=vmem,
         scratch_shapes=[
             pltpu.VMEM((rows, width), BF16),
             pltpu.VMEM((3, ada_weight.shape[0], columns), BF16),
             pltpu.VMEM((3, width, inner), BF16),
-            pltpu.VMEM((inner, width), BF16),
+            pltpu.VMEM((parts, inner, columns), BF16),
             pltpu.VMEM((rows, width), F32),
             pltpu.VMEM((rows, width), BF16),
             pltpu.VMEM((parts, 8, columns), F32),
-            pltpu.VMEM((n, 8, columns), F32),
+            pltpu.VMEM((n, 1, columns), F32),
             pltpu.VMEM((n, slab, columns), BF16),
             pltpu.VMEM((n, 2, rows, inner), BF16),
             pltpu.VMEM((rows, inner), BF16),
             pltpu.VMEM((n, slab, inner), BF16),
             pltpu.VMEM((rows, inner), F32),
             pltpu.VMEM((rows, inner), F32),
-            pltpu.VMEM((rows + slab, inner), BF16),
-            pltpu.VMEM((parts, rows + slab, columns), BF16),
-            pltpu.VMEM((parts, rows + slab, columns), BF16),
-            pltpu.VMEM((rows + slab, columns), F32),
+            pltpu.VMEM((parts, rows + slab, inner), BF16),
             dma((6,)), dma((parts,)), dma((parts,)), dma((n,)), dma((n,)), dma((n,)), dma((n,)),
             dma((2, 3, n)), dma((2, n)), dma((n,)), dma((n,)), dma((parts,)), dma((parts,)),
+            dma((parts,)), dma((parts,)),
         ],
         compiler_params=pltpu.CompilerParams(
             collective_id=0, has_side_effects=True, vmem_limit_bytes=60 * 1024 * 1024
         ),
     )(
-        head_slot, embedding, gains, latents, fresh_noise,
+        head_slot, levels, q_gain.reshape(1, -1), k_gain.reshape(1, -1), latents,
         jnp.transpose(ada_weight, (1, 0, 2)), jnp.transpose(qkv_weight, (1, 0, 2)), out_weight,
     )
+    window, clean = pl.pallas_call(
+        functools.partial(finish_kernel, n),
+        out_shape=(
+            jax.ShapeDtypeStruct((rows, columns), BF16),
+            jax.ShapeDtypeStruct((slab, columns), BF16),
+        ),
+        in_specs=[smem, vmem, vmem],
+        out_specs=(vmem, vmem),
+    )(head_slot, updated, fresh_noise)
     if clean_rows < slab:
         start = (lax.axis_index("seq") * clean_rows) % slab
         clean = lax.dynamic_slice_in_dim(clean, start, clean_rows, 0)

time: 56.2 us -> 42.4 us (0.75)
  Pallas kernels: 49.2 us -> 40.3 us
  local copies, waits for them, and re-layouts: 2.93 us -> 0 us
  other arithmetic: 1.88 us -> 0 us
    pallas_call x1, Pallas kernels: 49.2 us -> 38.6 us  [local(): pl.pallas_call(functools.partial(kernel, n, parts, slab, clean_rows), out...]
    unnamed x2 -> x0, local copies, waits for them, and re-layouts: 2.93 us -> none
    pallas_call x0 -> x1, Pallas kernels: none -> 1.71 us  [local(): pl.pallas_call(functools.partial(finish_kernel, n), out_shape=(jax.ShapeD...]
    another operation x1 -> x0, other arithmetic: 1.24 us -> none  [local(): gains = jnp.stack([q_gain, k_gain])]
    convert_element_type x1 -> x0, other arithmetic: 0.59 us -> none  [embed(): jax.nn.silu(jnp.concatenate([jnp.cos(angles), jnp.sin(angles)], axis=1))]
where the time goes in v3:
time: 42.4 us; the launch traced here: 42.2 us
  Pallas kernels  40.3 us (95%)
  between operations  1.93 us (5%)
    pallas_call x1, Pallas kernels, local(): pl.pallas_call(functools.partial(kernel, n, parts, slab, clean_rows), out...  38.6 us
    pallas_call x1, Pallas kernels, local(): pl.pallas_call(functools.partial(finish_kernel, n), out_shape=(jax.ShapeD...  1.71 us

profile of v3, /device:TPU:1, one launch (start us, length us, event | category | flops | bytes accessed | tf_op | source)
XLA Modules:
  0.0 42.2 jit_solution(16359619298646958112)
XLA Ops:
  1.9 38.6 %shard_map.104.updated_ref = bf16[144,640]{1,0:T(8,128)(2,1)} custom-call(s32[1]{0:T(128)S(6)} %copy.12.head_ref, s32[1]{0:T(128)S(6)} %copy.11.level_ref, f32[1,128]{1,0:T(1,128)} %bitcast.6, f32[1,128]{1,0:T(1,128)} %bitcast.7, bf16[128,2560]{1,0:T(8,128)(2,1)} %lat_hbm.1, bf16[3,256,640]{2,1,0:T(8,128)(2,1)} %bitcast.5, bf16[3,2560,384]{2,1,0:T(8,128)(2,1)} %bitcast.4, ...), custom_call_target="tpu_custom_call" | custom-call | tf_op jit(solution)/shard_map/pallas_call | solution.py:393
  40.5 1.7 %shard_map.105 = (bf16[128,640]{1,0:T(8,128)(2,1)}, bf16[16,640]{1,0:T(8,128)(2,1)}) custom-call(s32[1]{0:T(128)S(6)} %copy.12.head_ref, bf16[144,640]{1,0:T(8,128)(2,1)} %shard_map.104.updated_ref, bf16[128,640]{1,0:T(8,128)(2,1)} %noise_ref.1), custom_call_target="tpu_custom_call" | custom-call | tf_op jit(solution)/shard_map/pallas_call | solution.py:427

commit v4 on v3

--- a/solution.py
+++ b/solution.py
@@ -23,9 +23,9 @@
 
 def kernel(
     n, parts, slab, clean_rows,
-    head_ref, level_ref, q_gain_ref, k_gain_ref, lat_hbm, ada_hbm, qkv_hbm, out_hbm,
+    head_hbm, level_hbm, q_gain_hbm, k_gain_hbm, noise_hbm, lat_hbm, ada_hbm, qkv_hbm, out_hbm,
     updated_ref,
-    lat, ada, wqkv, wout, normed, hidden, mods, gates, lat_rows, kv, queries, q_rows,
+    head_ref, level_ref, q_gain_ref, k_gain_ref, noise, lat, ada, wqkv, wout, normed, hidden, mods, gates, lat_rows, kv, queries, q_rows,
     acc, totals, attended,
     load_sem, mod_send, mod_recv, gate_send, gate_recv, row_send, row_recv,
     kv_send, kv_recv, q_send, q_recv, w_send, w_recv, att_send, att_recv,
@@ -55,7 +55,17 @@
             out_hbm.at[:, pl.ds(pl.multiple_of(part * columns, 128), columns)],
             wout.at[part], load_sem.at[5],
         ),
+        pltpu.make_async_copy(noise_hbm, noise, load_sem.at[6]),
     ]
+    small = [
+        pltpu.make_async_copy(source, held, load_sem.at[7 + index])
+        for index, (source, held) in enumerate((
+            (level_hbm, level_ref), (head_hbm, head_ref),
+            (q_gain_hbm, q_gain_ref), (k_gain_hbm, k_gain_ref),
+        ))
+    ]
+    for load in small:
+        load.start()
     for load in loads:
         load.start()
 
@@ -73,6 +83,8 @@
             device_id_type=pl.DeviceIdType.MESH,
         )
 
+    for load in small:
+        load.wait()
     half_width = ada.shape[1] // 2
     order = lax.broadcasted_iota(jnp.int32, (16, half_width), 1).astype(F32)
     angles = level_ref[0].astype(F32) * jnp.exp(-math.log(10000.0) * order / half_width)
@@ -329,7 +341,10 @@
         total = add(handed, total)
 
     own_states = lat[:, pl.ds(first_column, columns)].astype(F32)
-    updated_ref[0:rows, :] = (own_states + gates[me] * total[0:rows]).astype(BF16)
+    updated = (own_states + gates[me] * total[0:rows]).astype(BF16)
+    leaving = jnp.full((rows, columns), own_rank, jnp.int32) == 0
+    loads[6].wait()
+    updated_ref[0:rows, :] = jnp.where(leaving, noise[...], updated)
     updated_ref[rows:, :] = (
         lat_rows[oldest].astype(F32) + gates[oldest] * total[rows:]
     ).astype(BF16)
@@ -368,11 +383,9 @@
                 onward(kind, above, 2, finish)
 
 
-def finish_kernel(n, head_ref, updated_ref, noise_ref, window_ref, clean_ref):
+def finish_kernel(updated_ref, window_ref, clean_ref):
     rows = window_ref.shape[0]
-    own_rank = lax.rem(lax.axis_index("seq") - head_ref[0] + n, n)
-    leaving = jnp.full(window_ref.shape, own_rank, jnp.int32) == 0
-    window_ref[...] = jnp.where(leaving, noise_ref[...], updated_ref[0:rows, :])
+    window_ref[...] = updated_ref[0:rows, :]
     clean_ref[...] = updated_ref[rows:, :]
 
 
@@ -387,17 +400,21 @@
     clean_rows = rows // n
     slab = max(clean_rows, 16)
     vmem = pl.BlockSpec(memory_space=pltpu.VMEM)
-    smem = pl.BlockSpec(memory_space=pltpu.SMEM)
-    hbm = pl.BlockSpec(memory_space=pl.ANY)
+    hbm = pl.BlockSpec(memory_space=pltpu.HBM)
     dma = pltpu.SemaphoreType.DMA
     updated = pl.pallas_call(
         functools.partial(kernel, n, parts, slab, clean_rows),
         out_shape=jax.ShapeDtypeStruct((rows + slab, columns), BF16),
         in_specs=[
-            smem, smem, vmem, vmem, hbm, hbm, hbm, hbm,
+            hbm, hbm, hbm, hbm, hbm, hbm, hbm, hbm, hbm,
         ],
         out_specs=vmem,
         scratch_shapes=[
+            pltpu.SMEM((1,), jnp.int32),
+            pltpu.SMEM((1,), jnp.int32),
+            pltpu.VMEM((1, q_gain.shape[0]), F32),
+            pltpu.VMEM((1, q_gain.shape[0]), F32),
+            pltpu.VMEM((rows, columns), BF16),
             pltpu.VMEM((rows, width), BF16),
             pltpu.VMEM((3, ada_weight.shape[0], columns), BF16),
             pltpu.VMEM((3, width, inner), BF16),
@@ -413,7 +430,7 @@
             pltpu.VMEM((rows, inner), F32),
             pltpu.VMEM((rows, inner), F32),
             pltpu.VMEM((parts, rows + slab, inner), BF16),
-            dma((6,)), dma((parts,)), dma((parts,)), dma((n,)), dma((n,)), dma((n,)), dma((n,)),
+            dma((11,)), dma((parts,)), dma((parts,)), dma((n,)), dma((n,)), dma((n,)), dma((n,)),
             dma((2, 3, n)), dma((2, n)), dma((n,)), dma((n,)), dma((parts,)), dma((parts,)),
             dma((parts,)), dma((parts,)),
         ],
@@ -421,18 +438,18 @@
             collective_id=0, has_side_effects=True, vmem_limit_bytes=60 * 1024 * 1024
         ),
     )(
-        head_slot, levels, q_gain.reshape(1, -1), k_gain.reshape(1, -1), latents,
+        head_slot, levels, q_gain.reshape(1, -1), k_gain.reshape(1, -1), fresh_noise, latents,
         jnp.transpose(ada_weight, (1, 0, 2)), jnp.transpose(qkv_weight, (1, 0, 2)), out_weight,
     )
     window, clean = pl.pallas_call(
-        functools.partial(finish_kernel, n),
+        finish_kernel,
         out_shape=(
             jax.ShapeDtypeStruct((rows, columns), BF16),
             jax.ShapeDtypeStruct((slab, columns), BF16),
         ),
-        in_specs=[smem, vmem, vmem],
+        in_specs=[vmem],
         out_specs=(vmem, vmem),
-    )(head_slot, updated, fresh_noise)
+    )(updated)
     if clean_rows < slab:
         start = (lax.axis_index("seq") * clean_rows) % slab
         clean = lax.dynamic_slice_in_dim(clean, start, clean_rows, 0)

time: 42.4 us -> 41.8 us (0.986)
  Pallas kernels: 40.3 us -> 39.7 us
    pallas_call x1, Pallas kernels: 38.6 us -> 38 us  [local(): pl.pallas_call(functools.partial(kernel, n, parts, slab, clean_rows), out...]
where the time goes in v4:
time: 41.8 us; the launch traced here: 41.6 us
  Pallas kernels  39.7 us (95%)
  between operations  1.93 us (5%)
    pallas_call x1, Pallas kernels, local(): pl.pallas_call(functools.partial(kernel, n, parts, slab, clean_rows), out...  38 us
    pallas_call x1, Pallas kernels, local(): pl.pallas_call(finish_kernel, out_shape=(jax.ShapeDtypeStruct((rows, colu...  1.61 us

profile of v4, /device:TPU:1, one launch (start us, length us, event | category | flops | bytes accessed | tf_op | source)
XLA Modules:
  0.0 41.6 jit_solution(5494650961442272543)
XLA Ops:
  1.9 38.0 %shard_map.104.updated_ref = bf16[144,640]{1,0:T(8,128)(2,1)} custom-call(s32[1]{0:T(128)S(6)} %copy.12.head_hbm, s32[1]{0:T(128)S(6)} %copy.11.level_hbm, f32[1,128]{1,0:T(1,128)} %bitcast.6, f32[1,128]{1,0:T(1,128)} %bitcast.7, bf16[128,640]{1,0:T(8,128)(2,1)} %noise_hbm.1, bf16[128,2560]{1,0:T(8,128)(2,1)} %lat_hbm.1, bf16[3,256,640]{2,1,0:T(8,128)(2,1)} %bitcast.5, ...), custom_call_target="tpu_custom_call" | custom-call | tf_op jit(solution)/shard_map/pallas_call | solution.py:405
  40.0 1.6 %shard_map.105 = (bf16[128,640]{1,0:T(8,128)(2,1)}, bf16[16,640]{1,0:T(8,128)(2,1)}) custom-call(bf16[144,640]{1,0:T(8,128)(2,1)} %shard_map.104.updated_ref), custom_call_target="tpu_custom_call" | custom-call | tf_op jit(solution)/shard_map/pallas_call | solution.py:444

commit v5 on v4

--- a/solution.py
+++ b/solution.py
@@ -34,6 +34,7 @@
     part = lax.axis_index("tensor")
     pair = 2
     side = lax.rem(me, pair)
+    mate = me + pair * (1 - 2 * lax.rem(me // pair, 2))
     rows, width = lat.shape
     columns = updated_ref.shape[1]
     head_size = q_gain_ref.shape[1]
@@ -178,6 +179,12 @@
         else:
             pl.when(there)(run)
 
+    def hand_across(kind, slot, act):
+        if kind == 0:
+            onward(kind, slot, 2, act)
+        else:
+            pl.when(slot != mate)(lambda: onward(kind, slot, 2, act))
+
     def start(kind, slot, way, target):
         kv_copy(kind, slot, way, target).start()
 
@@ -255,17 +262,20 @@
             def _():
                 kv_copy(kind, below, 1, me).wait_recv()
                 onward(kind, below, 1, start)
-                onward(kind, below, 2, start)
+                hand_across(kind, below, start)
 
             @pl.when(above < n)
             def _():
                 kv_copy(kind, above, 0, me).wait_recv()
                 onward(kind, above, 0, start)
-                onward(kind, above, 2, start)
+                hand_across(kind, above, start)
 
         @pl.when(step == 1)
         def _():
-            take_across(other)
+            kv_copy(1, other, 0, me).wait_recv()
+            kv_copy(1, other, 0, mate).start()
+            kv_copy(0, other, 2, me).wait_recv()
+            absorb(other)
 
         @pl.when((step > 1) & (other - (step - 1) * pair >= 0))
         def _():
@@ -363,6 +373,7 @@
         gate_copy(me, target).wait_send()
         row_copy(me, target).wait_send()
 
+    kv_copy(1, other, 0, mate).wait_send()
     for kind in range(2):
         for way in range(3):
             onward(kind, me, way, finish)
@@ -375,12 +386,12 @@
             @pl.when(below >= 0)
             def _():
                 onward(kind, below, 1, finish)
-                onward(kind, below, 2, finish)
+                hand_across(kind, below, finish)
 
             @pl.when(above < n)
             def _():
                 onward(kind, above, 0, finish)
-                onward(kind, above, 2, finish)
+                hand_across(kind, above, finish)
 
 
 def finish_kernel(updated_ref, window_ref, clean_ref):

time: 41.8 us -> 43.7 us (1.045)
  Pallas kernels: 39.7 us -> 41.6 us
    pallas_call x1, Pallas kernels: 38 us -> 40 us  [local(): pl.pallas_call(functools.partial(kernel, n, parts, slab, clean_rows), out...]
where the time goes in v5:
time: 43.7 us; the launch traced here: 43.5 us
  Pallas kernels  41.6 us (95%)
  between operations  1.93 us (4%)
    pallas_call x1, Pallas kernels, local(): pl.pallas_call(functools.partial(kernel, n, parts, slab, clean_rows), out...  40 us
    pallas_call x1, Pallas kernels, local(): pl.pallas_call(finish_kernel, out_shape=(jax.ShapeDtypeStruct((rows, colu...  1.61 us

profile of v5, /device:TPU:1, one launch (start us, length us, event | category | flops | bytes accessed | tf_op | source)
XLA Modules:
  0.0 43.5 jit_solution(14019519443078766098)
XLA Ops:
  1.9 40.0 %shard_map.104.updated_ref = bf16[144,640]{1,0:T(8,128)(2,1)} custom-call(s32[1]{0:T(128)S(6)} %copy.12.head_hbm, s32[1]{0:T(128)S(6)} %copy.11.level_hbm, f32[1,128]{1,0:T(1,128)} %bitcast.6, f32[1,128]{1,0:T(1,128)} %bitcast.7, bf16[128,640]{1,0:T(8,128)(2,1)} %noise_hbm.1, bf16[128,2560]{1,0:T(8,128)(2,1)} %lat_hbm.1, bf16[3,256,640]{2,1,0:T(8,128)(2,1)} %bitcast.5, ...), custom_call_target="tpu_custom_call" | custom-call | tf_op jit(solution)/shard_map/pallas_call | solution.py:416
  41.9 1.6 %shard_map.105 = (bf16[128,640]{1,0:T(8,128)(2,1)}, bf16[16,640]{1,0:T(8,128)(2,1)}) custom-call(bf16[144,640]{1,0:T(8,128)(2,1)} %shard_map.104.updated_ref), custom_call_target="tpu_custom_call" | custom-call | tf_op jit(solution)/shard_map/pallas_call | solution.py:455

commit v6 on v5

--- a/solution.py
+++ b/solution.py
@@ -252,6 +252,7 @@
         absorb(source)
 
     other = me + 1 - 2 * side
+    mate_other = mate + 1 - 2 * side
 
     @pl.loop(1, n // pair)
     def _(step):
@@ -272,18 +273,21 @@
 
         @pl.when(step == 1)
         def _():
-            kv_copy(1, other, 0, me).wait_recv()
+            take_across(other)
+
+        @pl.when(step == min(2, n // pair - 1))
+        def _():
             kv_copy(1, other, 0, mate).start()
-            kv_copy(0, other, 2, me).wait_recv()
-            absorb(other)
-
-        @pl.when((step > 1) & (other - (step - 1) * pair >= 0))
-        def _():
-            take_across(other - (step - 1) * pair)
-
-        @pl.when((step > 1) & (other + (step - 1) * pair < n))
-        def _():
-            take_across(other + (step - 1) * pair)
+
+        before, after = other - (step - 1) * pair, other + (step - 1) * pair
+
+        @pl.when((step > 1) & (before >= 0) & (before != mate_other))
+        def _():
+            take_across(before)
+
+        @pl.when((step > 1) & (after < n) & (after != mate_other))
+        def _():
+            take_across(after)
 
         @pl.when(below >= 0)
         def _():
@@ -295,13 +299,15 @@
 
     last = n - pair
 
-    @pl.when(other - last >= 0)
+    @pl.when((other - last >= 0) & (other - last != mate_other))
     def _():
         take_across(other - last)
 
-    @pl.when(other + last < n)
+    @pl.when((other + last < n) & (other + last != mate_other))
     def _():
         take_across(other + last)
+
+    take_across(mate_other)
 
     @pl.loop(1, n)
     def _(step):

time: 43.7 us -> 42.4 us (0.970)
  Pallas kernels: 41.6 us -> 40.3 us
    pallas_call x1, Pallas kernels: 40 us -> 38.7 us  [local(): pl.pallas_call(functools.partial(kernel, n, parts, slab, clean_rows), out...]
where the time goes in v6:
time: 42.4 us; the launch traced here: 42.2 us
  Pallas kernels  40.3 us (95%)
  between operations  1.93 us (5%)
    pallas_call x1, Pallas kernels, local(): pl.pallas_call(functools.partial(kernel, n, parts, slab, clean_rows), out...  38.7 us
    pallas_call x1, Pallas kernels, local(): pl.pallas_call(finish_kernel, out_shape=(jax.ShapeDtypeStruct((rows, colu...  1.61 us

profile of v6, /device:TPU:1, one launch (start us, length us, event | category | flops | bytes accessed | tf_op | source)
XLA Modules:
  0.0 42.2 jit_solution(13109722316985140990)
XLA Ops:
  1.9 38.7 %shard_map.104.updated_ref = bf16[144,640]{1,0:T(8,128)(2,1)} custom-call(s32[1]{0:T(128)S(6)} %copy.12.head_hbm, s32[1]{0:T(128)S(6)} %copy.11.level_hbm, f32[1,128]{1,0:T(1,128)} %bitcast.6, f32[1,128]{1,0:T(1,128)} %bitcast.7, bf16[128,640]{1,0:T(8,128)(2,1)} %noise_hbm.1, bf16[128,2560]{1,0:T(8,128)(2,1)} %lat_hbm.1, bf16[3,256,640]{2,1,0:T(8,128)(2,1)} %bitcast.5, ...), custom_call_target="tpu_custom_call" | custom-call | tf_op jit(solution)/shard_map/pallas_call | solution.py:422
  40.6 1.6 %shard_map.105 = (bf16[128,640]{1,0:T(8,128)(2,1)}, bf16[16,640]{1,0:T(8,128)(2,1)}) custom-call(bf16[144,640]{1,0:T(8,128)(2,1)} %shard_map.104.updated_ref), custom_call_target="tpu_custom_call" | custom-call | tf_op jit(solution)/shard_map/pallas_call | solution.py:461
